TPU v7x, 128 devices: a whole 4x4x4 slice. The times are simulated.
128 devices in a mesh: dp: 8 (over x, core), adapter: 16 (over z, y).
Axes of the slice: x: 4, y: 4, z: 4, core: 2. Of those that a mesh axis runs over, the one named last changes fastest.
Arguments:
- residual_input: bfloat16 [65536, 2560], P(('dp', 'adapter')), may hold values from -6 to 6
- input_norm_gain: float32 [2560], replicated, may hold values from 0.5 to 1.5
- base_projection_weight: bfloat16 [2560, 4096], P('adapter', 'dp'), may hold values from -0.125 to 0.125
- query_key_gains: float32 [2, 256], replicated, may hold values from 0.5 to 1.5
- adapter_down_weight: bfloat16 [64, 2560, 48], P('adapter'), may hold values from -0.125 to 0.125
- adapter_up_weight: bfloat16 [64, 16, 4096], P('adapter'), may hold values from -1.5 to 1.5
- row_adapter_index: int32 [65536, 1], P(('dp', 'adapter')), may hold values from 0 to 63; in each aligned block of 512 rows (0 to 511, 512 to 1023, ...) at most 16 rows name the same one
- row_sequence_index: int32 [65536], P(('dp', 'adapter')), may hold values from 0 to 7, never falling along the last dimension, each value on 1 to 12288 neighbouring positions
Outputs:
- attended: bfloat16 [65536, 2048], P(('dp', 'adapter'))
Inputs may be any that keep to these rules, and one draw needn't show every extreme that they name: `row_adapter_index`: among the rows of one device, no adapter serves more than 16 rows; some adapter serves exactly 16 rows of some device. `row_sequence_index`: sequence numbers never fall along the rows; every sequence has 1 to 12288 rows, one exactly 12288.
All inputs are finite; a program needn't handle non-finite values.
Results may differ from a plain program's by a relative error of at most 0.02.
Values may be sent and summed in bfloat16 or wider, within the bound.
A program may use at most 128 MiB of HBM per device.

v0:
```python
import jax
import jax.numpy as jnp
from jax import lax
from jax.sharding import PartitionSpec as P

HEADS = 8
KV_HEADS = 4
HEAD_DIM = 256
WINDOW = 1024


def shifted(value, axis, by):
    size = lax.axis_size(axis)
    pairs = [(i, i + by) for i in range(size) if 0 <= i + by < size]
    return lax.ppermute(value, axis, pairs)


def head_norm(block, heads, gain):
    shaped = block.reshape(block.shape[0], heads, HEAD_DIM)
    scaled = shaped * lax.rsqrt(jnp.mean(shaped * shaped, axis=-1, keepdims=True) + 1e-06) * gain
    return scaled.astype(jnp.bfloat16)


def adapter_delta(rank_values, up_matrices):
    width_q = HEADS * HEAD_DIM
    width_k = KV_HEADS * HEAD_DIM
    inner = up_matrices.shape[1]
    part_q = jnp.einsum(
        "nacr,arq->nacq",
        rank_values[..., 0:inner],
        up_matrices[:, :, 0:width_q],
        preferred_element_type=jnp.float32,
    )
    part_k = jnp.einsum(
        "nacr,arq->nacq",
        rank_values[..., inner : 2 * inner],
        up_matrices[:, :, width_q : width_q + width_k],
        preferred_element_type=jnp.float32,
    )
    part_v = jnp.einsum(
        "nacr,arq->nacq",
        rank_values[..., 2 * inner : 3 * inner],
        up_matrices[:, :, width_q + width_k :],
        preferred_element_type=jnp.float32,
    )
    return jnp.concatenate([part_q, part_k, part_v], axis=-1).astype(jnp.bfloat16)


def adapter_ranks(adapter_slots, down_matrices):
    return jnp.einsum(
        "nacd,adr->nacr", adapter_slots, down_matrices, preferred_element_type=jnp.float32
    ).astype(jnp.bfloat16)


def body(
    residual_input,
    input_norm_gain,
    base_projection_weight,
    query_key_gains,
    adapter_down_weight,
    adapter_up_weight,
    row_adapter_index,
    row_sequence_index,
):
    rows = residual_input.shape[0]
    width = residual_input.shape[1]
    width_q = HEADS * HEAD_DIM
    width_k = KV_HEADS * HEAD_DIM
    group = HEADS // KV_HEADS
    values_in = residual_input.astype(jnp.float32)
    normed = (
        values_in
        * lax.rsqrt(jnp.mean(values_in * values_in, axis=-1, keepdims=True) + 1e-06)
        * input_norm_gain
    ).astype(jnp.bfloat16)
    slab = lax.all_gather(base_projection_weight, "dp", axis=1, tiled=True)
    base = jnp.dot(
        normed,
        lax.all_gather(slab, "adapter", axis=0, tiled=True),
        preferred_element_type=jnp.float32,
    ).astype(jnp.bfloat16)
    total_width = base.shape[1]
    owners = lax.axis_size("adapter")
    local_adapter_count = adapter_down_weight.shape[0]
    adapters_all = owners * local_adapter_count
    capacity = 2 * rows // adapters_all
    adapter_ids = row_adapter_index[:, 0]
    onehot = (adapter_ids[:, None] == jnp.arange(adapters_all, dtype=jnp.int32)[None, :]).astype(
        jnp.int32
    )
    earlier = jnp.cumsum(onehot, axis=0) - onehot
    place = jnp.sum(earlier * onehot, axis=1)
    slot = adapter_ids * capacity + place
    scratch_buffer = jnp.zeros((adapters_all * capacity, width), jnp.bfloat16).at[slot].set(normed)
    scratch_buffer = scratch_buffer.reshape(owners, local_adapter_count, capacity, width)
    adapter_corrections = adapter_delta(
        adapter_ranks(
            lax.all_to_all(scratch_buffer, "adapter", split_axis=0, concat_axis=0, tiled=True),
            adapter_down_weight,
        ),
        adapter_up_weight,
    )
    returned = lax.all_to_all(
        adapter_corrections, "adapter", split_axis=0, concat_axis=0, tiled=True
    )
    delta_slots = returned.reshape(adapters_all * capacity, total_width)
    delta_update = delta_slots[slot]
    projected = base.astype(jnp.float32) + delta_update.astype(jnp.float32)
    queries = head_norm(projected[:, 0:width_q], HEADS, query_key_gains[0]).reshape(
        rows, KV_HEADS, group, HEAD_DIM
    )
    keys = head_norm(
        projected[:, width_q : width_q + width_k], KV_HEADS, query_key_gains[1]
    ).reshape(rows, width_k)
    values = projected[:, width_q + width_k :].astype(jnp.bfloat16)
    before = (WINDOW + rows - 2) // rows
    key_parts = []
    value_parts = []
    seg_parts = []
    for offset in range(before, 0, -1):
        moved_keys, moved_values, moved_seg = shifted(
            (keys, values, row_sequence_index), ("dp", "adapter"), offset
        )
        key_parts.append(moved_keys)
        value_parts.append(moved_values)
        seg_parts.append(moved_seg)
    key_parts.append(keys)
    value_parts.append(values)
    seg_parts.append(row_sequence_index)
    span = (before + 1) * rows
    key_all = jnp.concatenate(key_parts, axis=0).reshape(span, KV_HEADS, HEAD_DIM)
    value_all = jnp.concatenate(value_parts, axis=0).reshape(span, KV_HEADS, HEAD_DIM)
    seg_all = jnp.concatenate(seg_parts, axis=0)
    position = lax.axis_index(("dp", "adapter"))
    query_pos = position * rows + jnp.arange(rows, dtype=jnp.int32)
    key_pos = (position - before) * rows + jnp.arange(span, dtype=jnp.int32)
    gap = query_pos[:, None] - key_pos[None, :]
    allowed = (
        (row_sequence_index[:, None] == seg_all[None, :])
        & (gap >= 0)
        & (gap < WINDOW)
        & (key_pos[None, :] >= 0)
    )
    scores = jnp.einsum(
        "tkgd,skd->kgts", queries, key_all, preferred_element_type=jnp.float32
    ) * HEAD_DIM ** (-0.5)
    weights = jnp.where(allowed[None, None], jnp.exp(scores), jnp.float32(0.0))
    total = jnp.sum(weights, axis=-1)
    probs = weights.astype(jnp.bfloat16)
    summed = jnp.einsum("kgts,skd->tkgd", probs, value_all, preferred_element_type=jnp.float32)
    result = summed / jnp.transpose(total, (2, 0, 1))[..., None]
    return result.reshape(rows, width_q).astype(jnp.bfloat16)


def solution(mesh):
    placed = (
        P(("dp", "adapter"), None),
        P(),
        P("adapter", "dp"),
        P(),
        P("adapter", None, None),
        P("adapter", None, None),
        P(("dp", "adapter"), None),
        P(("dp", "adapter")),
    )
    return jax.shard_map(
        body, mesh=mesh, in_specs=placed, out_specs=P(("dp", "adapter"), None), check_vma=False
    )
```

profile of v0, /device:TPU:3, one launch (start us, length us, event | category | flops | bytes accessed | tf_op | source)
XLA Modules:
  0.0 495.9 jit_solution(7275896673530061145)
XLA Ops:
  7.3 26.8 %all-gather.3.cloned.1.call-done = bf16[160,4096]{1,0:T(8,128)(2,1)} async-done(((bf16[160,512]{1,0:T(8,128)(2,1)}), bf16[160,4096]{1,0:T(8,128)(2,1)}) %all-gather.3.cloned.1.call-update) | async-done | bytes 1310736 | tf_op jit(solution)/shard_map/all_gather | solution.py:76
  39.5 9.0 %scatter_custom_fusion = bf16[1024,2560]{1,0:T(8,128)(2,1)} fusion(s32[512]{0:T(512)S(1)} %bitcast.120, bf16[]{:T(256)} %constant.17.clone.1, bf16[512,2560]{1,0:T(8,128)(2,1)} %param.8, f32[2560]{0:T(1024)S(1)} %copy-done.8, f32[512]{0:T(512)S(1)} %add_rsqrt_fusion.2), kind=kCustom, calls=%fused_computation.37 | custom fusion | flops 5242880 | bytes 7878658 | tf_op jit(solution)/shard_map/scatter | solution.py:94
  48.5 83.8 %all_to_all.10 = bf16[16,4,16,2560]{3,2,1,0:T(8,128)(2,1)S(1)} all-to-all(bf16[16,4,16,2560]{3,2,1,0:T(8,128)(2,1)} %bitcast.105), channel_id=1, replica_groups=mesh['dp'=8,'adapter'=16] {'adapter'}, dimensions={0} | all-to-all | bytes 10485760 | tf_op jit(solution)/shard_map/all_to_all | solution.py:98
  136.6 4.3 pad_maximum_fusion
  140.9 8.3 %copy.62 = bf16[16,4,16,4096]{3,2,1,0:T(8,128)(2,1)} copy(bf16[16,4,16,4096]{3,2,0,1:T(8,128)(2,1)} %pad_maximum_fusion) | data formatting | bytes 16777216 | tf_op jit(solution)/shard_map/concatenate | solution.py:46
  149.2 5.1 %all-to-all-start.1 = ((bf16[16,4,16,4096]{3,2,1,0:T(8,128)(2,1)}), bf16[16,4,16,4096]{3,2,1,0:T(8,128)(2,1)}, u32[]{:S(2)}, u32[]{:S(2)}) async-start(bf16[16,4,16,4096]{3,2,1,0:T(8,128)(2,1)} %copy.62), calls=%async_computation.1 | async-start | bytes 16777216 | tf_op jit(solution)/shard_map/all_to_all | solution.py:103
  154.3 3.1 collective-permute-start.3
  157.4 4.3 collective-permute-start.2
  161.8 151.0 %collective-permute-done.3 = s32[512]{0:T(512)S(1)} collective-permute-done((s32[512]{0:T(512)S(1)}, s32[512]{0:T(512)S(1)}, u32[]{:S(2)}, u32[]{:S(2)}) %collective-permute-start.3) | collective-permute-done | bytes 2080 | tf_op jit(solution)/shard_map/ppermute | solution.py:15
  312.8 15.8 %collective-permute-done.2 = s32[512]{0:T(512)S(1)} collective-permute-done((s32[512]{0:T(512)S(1)}, s32[512]{0:T(512)S(1)}, u32[]{:S(2)}, u32[]{:S(2)}) %collective-permute-start.2) | collective-permute-done | bytes 2080 | tf_op jit(solution)/shard_map/ppermute | solution.py:15
  328.6 2.5 fusion.22
  331.1 13.0 %gather_fusion = bf16[512,4096]{1,0:T(8,128)(2,1)} fusion(bf16[1024,4096]{1,0:T(8,128)(2,1)} %bitcast.18, s32[1024]{0:T(1024)S(1)} %pad_clamp_fusion), kind=kCustom, calls=%fused_computation | custom fusion | bytes 8390656 | tf_op jit(solution)/shard_map/gather | solution.py:107
  344.1 16.6 %convert_add_fusion = f32[512,4096]{1,0:T(8,128)S(1)} fusion(bf16[512,4096]{1,0:T(8,128)(2,1)} %gather_fusion, bf16[2560,4096]{1,0:T(8,128)(2,1)} %all-gather.5.cloned.1.call-done, bf16[512,2560]{1,0:T(8,128)(2,1)} %param.8, f32[2560]{0:T(1024)S(1)} %copy-done.8, f32[512]{0:T(512)S(1)} %add_rsqrt_fusion.2), kind=kOutput, calls=%fused_computation.10 | convolution fusion | flops 10751049728 | bytes 36188160 | tf_op jit(solution)/shard_map/dot_general | solution.py:77
  375.7 3.1 collective-permute-start.4
  378.9 4.3 slice_multiply_fusion.1
  383.2 6.6 %reshape.168 = f32[512,4,2,256]{3,2,1,0:T(2,128)} reshape(f32[512,2048]{1,0:T(8,128)} %get-tuple-element.6) | data formatting | bytes 8388608 | tf_op jit(solution)/shard_map/reshape | solution.py:19
  389.8 6.1 %copy.87 = f32[64,8,8,256]{3,2,1,0:T(8,128)} copy(f32[64,8,8,256]{3,1,2,0:T(8,128)} %bitcast.106) | data formatting | bytes 8388608
  395.9 2.8 reduce_sum.51
  399.9 36.2 %collective-permute-done.1 = bf16[512,1024]{1,0:T(8,128)(2,1)} collective-permute-done((bf16[512,1024]{1,0:T(8,128)(2,1)}, bf16[512,1024]{1,0:T(8,128)(2,1)}, u32[]{:S(2)}, u32[]{:S(2)}) %collective-permute-start.1) | collective-permute-done | bytes 1048608 | tf_op jit(solution)/shard_map/ppermute | solution.py:15
  436.1 3.2 pad_maximum_fusion.1
  439.3 4.8 copy.80
  444.0 14.5 %collective-permute-done.5 = bf16[512,1024]{1,0:T(8,128)(2,1)} collective-permute-done((bf16[512,1024]{1,0:T(8,128)(2,1)S(1)}, bf16[512,1024]{1,0:T(8,128)(2,1)}, u32[]{:S(2)}, u32[]{:S(2)}) %collective-permute-start.5) | collective-permute-done | bytes 1048608 | tf_op jit(solution)/shard_map/ppermute | solution.py:15
  462.1 13.2 %fusion = (f32[4,2,512]{2,1,0:T(2,128)S(1)}, f32[4,1536,512,2]{2,1,3,0:T(8,128)}) fusion(pred[512,1536]{0,1:T(8,128)(4,1)S(1)} %copy-done.5, f32[512,4,2,256]{3,2,1,0:T(2,128)S(1)} %copy-done.4, f32[256]{0:T(256)S(1)} %bitcast.123, f32[512,4,2]{0,2,1:T(2,128)S(1)} %rsqrt.30, bf16[512,4,256]{2,0,1:T(8,128)(2,1)} %bitcast.113, ...), kind=kOutput, calls=%fused_computation.3 | convolution fusion | flops 3252678656 | bytes 33326080 | tf_op jit(solution)/shard_map/tkgd,skd->kgts/dot_general | solution.py:144
  475.3 11.4 %fusion.12 = bf16[512,4,2,256]{0,3,2,1:T(8,128)(2,1)S(1)} fusion(bf16[1536,4,256,1]{0,2,3,1:T(8,128)(2,1)} %bitcast.111, f32[4,1536,512,2]{2,1,3,0:T(8,128)} %get-tuple-element.10, pred[512,1536]{0,1:T(8,128)(4,1)} %fusion.22, f32[512,4,2]{0,2,1:T(2,128)S(1)} %bitcast.124), kind=kOutput, calls=%fused_computation.22 | convolution fusion | flops 3242196992 | bytes 31211520 | tf_op jit(solution)/shard_map/kgts,skd->tkgd/dot_general | solution.py:150
  (69 shorter events, 32.4 us)
Async XLA Ops:
  6.5 125.8 %copy-start = (bf16[4,2560,48]{1,2,0:T(8,128)(2,1)S(1)}, bf16[4,2560,48]{1,2,0:T(8,128)(2,1)}, u32[]{:S(2)}) copy-start(bf16[4,2560,48]{1,2,0:T(8,128)(2,1)} %param.12) | copy-start | bytes 2949124
  6.5 33.0 %copy-start.7 = (s32[512,1]{0,1:T(1,128)S(1)}, s32[512,1]{0,1:T(1,128)}, u32[]{:S(2)}) copy-start(s32[512,1]{0,1:T(1,128)} %param.14) | copy-start | bytes 6148
  6.5 33.0 %copy-start.8 = (f32[2560]{0:T(1024)S(1)}, f32[2560]{0:T(1024)}, u32[]{:S(2)}) copy-start(f32[2560]{0:T(1024)} %param.9) | copy-start | bytes 30724
  6.5 27.6 %all-gather.3.cloned.1.call-start = ((), (), s32[]{:S(2)}) async-start(), calls=%async_computation.2 | async-start | bytes 1474560 | tf_op jit(solution)/shard_map/all_gather | solution.py:76
  7.3 336.8 %all-gather.5.cloned.1.call-start = ((), (), s32[]{:S(2)}) async-start(), calls=%async_computation.3 | async-start | bytes 22282240 | tf_op jit(solution)/shard_map/all_gather | solution.py:79
  132.4 1.5 copy-start.6
  149.2 5.1 %copy-start.9 = (s32[512]{0:T(512)S(1)}, s32[512]{0:T(512)}, u32[]{:S(2)}) copy-start(s32[512]{0:T(512)} %param.15) | copy-start | bytes 6148
  149.2 12.6 %copy-start.10 = (f32[2,256]{1,0:T(2,128)S(1)}, f32[2,256]{1,0:T(2,128)}, u32[]{:S(2)}) copy-start(f32[2,256]{1,0:T(2,128)} %param.11) | copy-start | bytes 6148
  149.2 181.9 %all-to-all-start.1 = ((bf16[16,4,16,4096]{3,2,1,0:T(8,128)(2,1)}), bf16[16,4,16,4096]{3,2,1,0:T(8,128)(2,1)}, u32[]{:S(2)}, u32[]{:S(2)}) async-start(bf16[16,4,16,4096]{3,2,1,0:T(8,128)(2,1)} %copy.62), calls=%async_computation.1 | async-start | bytes 16777216 | tf_op jit(solution)/shard_map/all_to_all | solution.py:103
  154.3 158.5 %collective-permute-start.3 = (s32[512]{0:T(512)S(1)}, s32[512]{0:T(512)S(1)}, u32[]{:S(2)}, u32[]{:S(2)}) collective-permute-start(s32[512]{0:T(512)S(1)} %copy-done.9), channel_id=1, source_target_pairs={{0,1},{1,2},{2,3},{3,4},{4,5},{5,6},{6,7},{7,8},{8,9},{9,10},{10,1... | collective-permute-start | bytes 6152 | tf_op jit(solution)/shard_map/ppermute | solution.py:15
  157.4 171.2 %collective-permute-start.2 = (s32[512]{0:T(512)S(1)}, s32[512]{0:T(512)S(1)}, u32[]{:S(2)}, u32[]{:S(2)}) collective-permute-start(s32[512]{0:T(512)S(1)} %copy-done.9), channel_id=1, source_target_pairs={{0,2},{1,3},{2,4},{3,5},{4,6},{5,7},{6,8},{7,9},{8,10},{9,11},{10,... | collective-permute-start | bytes 6152 | tf_op jit(solution)/shard_map/ppermute | solution.py:15
  360.7 5.1 %copy-start.2 = (f32[512,4096]{1,0:T(8,128)}, f32[512,4096]{1,0:T(8,128)S(1)}, u32[]{:S(2)}) copy-start(f32[512,4096]{1,0:T(8,128)S(1)} %convert_add_fusion) | copy-start | bytes 25165828
  362.0 74.0 %collective-permute-start.1 = (bf16[512,1024]{1,0:T(8,128)(2,1)}, bf16[512,1024]{1,0:T(8,128)(2,1)}, u32[]{:S(2)}, u32[]{:S(2)}) collective-permute-start(bf16[512,1024]{1,0:T(8,128)(2,1)} %slice.85), channel_id=1, source_target_pairs={{0,1},{1,2},{2,3},{3,4},{4,5},{5,6},{6,7},{7,8},{8,9},{9,10},{10,1... | collective-permute-start | bytes 3145736 | tf_op jit(solution)/shard_map/ppermute | solution.py:15
  363.9 72.1 %collective-permute-start = (bf16[512,1024]{1,0:T(8,128)(2,1)}, bf16[512,1024]{1,0:T(8,128)(2,1)}, u32[]{:S(2)}, u32[]{:S(2)}) collective-permute-start(bf16[512,1024]{1,0:T(8,128)(2,1)} %slice.85), channel_id=1, source_target_pairs={{0,2},{1,3},{2,4},{3,5},{4,6},{5,7},{6,8},{7,9},{8,10},{9,11},{10,... | collective-permute-start | bytes 3145736 | tf_op jit(solution)/shard_map/ppermute | solution.py:15
  370.9 8.0 %copy-start.3 = (f32[512,4096]{1,0:T(8,128)S(1)}, f32[512,4096]{1,0:T(8,128)}, u32[]{:S(2)}) copy-start(f32[512,4096]{1,0:T(8,128)} %copy-done.2) | copy-start | bytes 25165828
  373.6 84.9 %collective-permute-start.5 = (bf16[512,1024]{1,0:T(8,128)(2,1)S(1)}, bf16[512,1024]{1,0:T(8,128)(2,1)}, u32[]{:S(2)}, u32[]{:S(2)}) collective-permute-start(bf16[512,1024]{1,0:T(8,128)(2,1)S(1)} %multiply_convert_fusion), channel_id=1, source_target_pairs={{0,1},{1,2},{2,3},{3,4},{4,5},{5,6},{6,7},{7,8},{8,9},{9,10},{10,1... | collective-permute-start | bytes 3145736 | tf_op jit(solution)/shard_map/ppermute | solution.py:15
  375.7 85.1 %collective-permute-start.4 = (bf16[512,1024]{1,0:T(8,128)(2,1)S(1)}, bf16[512,1024]{1,0:T(8,128)(2,1)}, u32[]{:S(2)}, u32[]{:S(2)}) collective-permute-start(bf16[512,1024]{1,0:T(8,128)(2,1)S(1)} %multiply_convert_fusion), channel_id=1, source_target_pairs={{0,2},{1,3},{2,4},{3,5},{4,6},{5,7},{6,8},{7,9},{8,10},{9,11},{10,... | collective-permute-start | bytes 3145736 | tf_op jit(solution)/shard_map/ppermute | solution.py:15
  439.3 22.8 %copy-start.5 = (pred[512,1536]{0,1:T(8,128)(4,1)S(1)}, pred[512,1536]{0,1:T(8,128)(4,1)}, u32[]{:S(2)}) copy-start(pred[512,1536]{0,1:T(8,128)(4,1)} %fusion.22) | copy-start | bytes 2359300
  444.0 18.1 %copy-start.4 = (f32[512,4,2,256]{3,2,1,0:T(2,128)S(1)}, f32[512,4,2,256]{3,2,1,0:T(2,128)}, u32[]{:S(2)}) copy-start(f32[512,4,2,256]{3,2,1,0:T(2,128)} %reshape.168) | copy-start | bytes 12582916
  475.3 13.8 %copy-start.1 = (bf16[4,2560,48]{1,2,0:T(8,128)(2,1)S(1)}, bf16[4,2560,48]{1,2,0:T(8,128)(2,1)}, u32[]{:S(2)}) copy-start(bf16[4,2560,48]{1,2,0:T(8,128)(2,1)} %param.12) | copy-start | bytes 2949124
Sparse Core Ops, SparseCore 0:
  9.1 25.0 all-gather.2
  36.3 278.7 all-gather.4
where the time goes:
time: 497 us; the launch traced here: 496 us
  waiting for transfers between devices  245 us (49%)
  blocking collectives  83.8 us (17%)
  local copies, waits for them, and re-layouts  50.7 us (10%)
  matrix products  45.4 us (9%)
  other arithmetic  35.7 us (7%)
  starting transfers between devices  21.5 us (4%)
  between operations  13.8 us (3%)
    ppermute x6, waiting for transfers between devices, shifted(): return lax.ppermute(value, axis, pairs)  217 us
    all_to_all x1, blocking collectives, body(): lax.all_to_all(scratch_buffer, 'adapter', split_axis=0, concat_axis=0, ti...  83.8 us
    all_gather x1, waiting for transfers between devices, body(): slab = lax.all_gather(base_projection_weight, 'dp', axis=1, tiled=True)  26.8 us
    dot_general x1, matrix products, body(): jnp.dot(normed, lax.all_gather(slab, 'adapter', axis=0, tiled=True), pref...  16.6 us
    ppermute x6, starting transfers between devices, shifted(): return lax.ppermute(value, axis, pairs)  16.4 us
    dot_general x1, matrix products, body(): jnp.einsum('tkgd,skd->kgts', queries, key_all, preferred_element_type=jnp...  13.2 us
    gather x1, local copies, waits for them, and re-layouts, body(): delta_update = delta_slots[slot]  13 us
    dot_general x1, matrix products, body(): jnp.einsum('kgts,skd->tkgd', probs, value_all, preferred_element_type=jnp...  11.4 us
  transfers between devices with their start and end apart: 9, of which 5 were waited for; matrix products, arithmetic and copies ran while one was open for 17% of the time, Pallas kernels for 0%

commit v1 on v0

--- a/solution.py
+++ b/solution.py
@@ -76,7 +76,9 @@
     slab = lax.all_gather(base_projection_weight, "dp", axis=1, tiled=True)
     base = jnp.dot(
         normed,
-        lax.all_gather(slab, "adapter", axis=0, tiled=True),
+        jnp.concatenate(
+            lax.all_to_all(jnp.stack([slab] * lax.axis_size("adapter")), "adapter", 0, 0), axis=0
+        ),
         preferred_element_type=jnp.float32,
     ).astype(jnp.bfloat16)
     total_width = base.shape[1]

time: 497 us -> 729 us (1.47)
  waiting for transfers between devices: 245 us -> 477 us
  blocking collectives: 83.8 us -> 68.8 us
  local copies, waits for them, and re-layouts: 50.7 us -> 59.6 us
    ppermute x6, waiting for transfers between devices: 217 us -> 356 us  [shifted(): return lax.ppermute(value, axis, pairs)]
    all_to_all x1, waiting for transfers between devices: 0.01 us -> 93 us  [body(): lax.all_to_all(adapter_corrections, 'adapter', split_axis=0, concat_axis=...]
    all_to_all x1, blocking collectives: 83.8 us -> 68.8 us  [body(): lax.all_to_all(scratch_buffer, 'adapter', split_axis=0, concat_axis=0, ti...]
    another operation x1 -> x2, local copies, waits for them, and re-layouts: 0.01 us -> 8.36 us  [the longest x1 8.35 us: body(): jnp.stack([slab] * lax.axis_size('adapter'))]
  transfers between devices with their start and end apart: 9 -> 9, of which waited for: 5 -> 7; matrix products, arithmetic and copies ran while one was open for 17% -> 5% of each run, Pallas kernels for 0% -> 0%
where the time goes in v1:
time: 729 us; the launch traced here: 726 us
  waiting for transfers between devices  477 us (65%)
  blocking collectives  68.8 us (9%)
  local copies, waits for them, and re-layouts  59.6 us (8%)
  matrix products  45.4 us (6%)
  other arithmetic  34 us (5%)
  starting transfers between devices  27.4 us (4%)
  between operations  13.7 us (2%)
    ppermute x6, waiting for transfers between devices, shifted(): return lax.ppermute(value, axis, pairs)  356 us
    all_to_all x1, waiting for transfers between devices, body(): lax.all_to_all(adapter_corrections, 'adapter', split_axis=0, concat_axis=...  93 us
    all_to_all x1, blocking collectives, body(): lax.all_to_all(scratch_buffer, 'adapter', split_axis=0, concat_axis=0, ti...  68.8 us
    all_gather x1, waiting for transfers between devices, body(): slab = lax.all_gather(base_projection_weight, 'dp', axis=1, tiled=True)  27.3 us
    ppermute x6, starting transfers between devices, shifted(): return lax.ppermute(value, axis, pairs)  17 us
    dot_general x1, matrix products, body(): jnp.dot(normed, jnp.concatenate(lax.all_to_all(jnp.stack([slab] * lax.axi...  16.8 us
  transfers between devices with their start and end apart: 9, of which 7 were waited for; matrix products, arithmetic and copies ran while one was open for 5% of the time, Pallas kernels for 0%

profile of v1, /device:TPU:3, one launch (start us, length us, event | category | flops | bytes accessed | tf_op | source)
XLA Modules:
  0.0 725.7 jit_solution(6210403250057828103)
XLA Ops:
  12.6 8.8 %scatter_custom_fusion = bf16[1024,2560]{1,0:T(8,128)(2,1)} fusion(s32[512]{0:T(512)S(1)} %bitcast.121, bf16[]{:T(256)} %constant.17.clone.1, bf16[512,2560]{1,0:T(8,128)(2,1)} %param.8, f32[2560]{0:T(1024)} %param.9, f32[512]{0:T(512)S(1)} %add_rsqrt_fusion.2), kind=kCustom, calls=%fused_computation.37 | custom fusion | flops 5242880 | bytes 7876610 | tf_op jit(solution)/shard_map/scatter | solution.py:96
  21.4 68.8 %all_to_all.15 = bf16[16,4,16,2560]{3,2,1,0:T(8,128)(2,1)S(1)} all-to-all(bf16[16,4,16,2560]{3,2,1,0:T(8,128)(2,1)} %bitcast.106), channel_id=1, replica_groups=mesh['dp'=8,'adapter'=16] {'adapter'}, dimensions={0} | all-to-all | bytes 10485760 | tf_op jit(solution)/shard_map/all_to_all | solution.py:100
  94.5 3.7 pad_maximum_fusion
  98.2 7.7 %copy.62 = bf16[16,4,16,4096]{3,2,1,0:T(8,128)(2,1)} copy(bf16[16,4,16,4096]{3,2,0,1:T(8,128)(2,1)} %pad_maximum_fusion) | data formatting | bytes 16777216 | tf_op jit(solution)/shard_map/concatenate | solution.py:46
  106.0 4.9 all-to-all-start.2
  111.7 27.3 %all-gather.2.cloned.1.call-done = bf16[160,4096]{1,0:T(8,128)(2,1)} async-done(((bf16[160,512]{1,0:T(8,128)(2,1)}), bf16[160,4096]{1,0:T(8,128)(2,1)}) %all-gather.2.cloned.1.call-update) | async-done | bytes 1310736 | tf_op jit(solution)/shard_map/all_gather | solution.py:76
  139.0 93.0 %all-to-all-done.2 = bf16[16,4,16,4096]{3,2,1,0:T(8,128)(2,1)} async-done(((bf16[16,4,16,4096]{3,2,1,0:T(8,128)(2,1)}), bf16[16,4,16,4096]{3,2,1,0:T(8,128)(2,1)}, u32[]{:S(2)}, u32[]{:S(2)}) %all-to-all-start.2) | async-done | bytes 8388640 | tf_op jit(solution)/shard_map/all_to_all | solution.py:105
  232.0 8.4 %stack.2 = bf16[16,160,4096]{2,1,0:T(8,128)(2,1)} broadcast(bf16[160,4096]{1,0:T(8,128)(2,1)} %all-gather.2.cloned.1.call-done), dimensions={1,2} | broadcast | bytes 22282240 | tf_op jit(solution)/shard_map/stack | solution.py:80
  240.3 5.5 all-to-all-start
  245.8 4.6 collective-permute-start.2
  252.7 298.8 %collective-permute-done.2 = s32[512]{0:T(512)S(1)} collective-permute-done((s32[512]{0:T(512)S(1)}, s32[512]{0:T(512)S(1)}, u32[]{:S(2)}, u32[]{:S(2)}) %collective-permute-start.2) | collective-permute-done | bytes 2080 | tf_op jit(solution)/shard_map/ppermute | solution.py:15
  551.5 13.1 %gather_fusion = bf16[512,4096]{1,0:T(8,128)(2,1)} fusion(bf16[1024,4096]{1,0:T(8,128)(2,1)} %bitcast.19, s32[1024]{0:T(1024)S(1)} %pad_clamp_fusion), kind=kCustom, calls=%fused_computation | custom fusion | bytes 8390656 | tf_op jit(solution)/shard_map/gather | solution.py:109
  564.7 16.8 %convert_add_fusion = f32[512,4096]{1,0:T(8,128)S(1)} fusion(bf16[512,4096]{1,0:T(8,128)(2,1)} %gather_fusion, bf16[2560,4096]{1,0:T(8,128)(2,1)} %bitcast, bf16[512,2560]{1,0:T(8,128)(2,1)} %param.8, f32[2560]{0:T(1024)S(1)} %copy-done.9, f32[512]{0:T(512)S(1)} %add_rsqrt_fusion.2), kind=kOutput, calls=%fused_computation.10 | convolution fusion | flops 10751049728 | bytes 36188160 | tf_op jit(solution)/shard_map/dot_general | solution.py:77
  581.5 3.2 copy-done.2
  609.1 3.9 copy.87
  616.0 6.6 reshape.174
  622.5 32.2 %collective-permute-done.5 = bf16[512,1024]{1,0:T(8,128)(2,1)} collective-permute-done((bf16[512,1024]{1,0:T(8,128)(2,1)S(1)}, bf16[512,1024]{1,0:T(8,128)(2,1)}, u32[]{:S(2)}, u32[]{:S(2)}) %collective-permute-start.5) | collective-permute-done | bytes 1048608 | tf_op jit(solution)/shard_map/ppermute | solution.py:15
  657.0 4.5 collective-permute-done.4
  663.9 8.9 %collective-permute-done = bf16[512,1024]{1,0:T(8,128)(2,1)} collective-permute-done((bf16[512,1024]{1,0:T(8,128)(2,1)S(1)}, bf16[512,1024]{1,0:T(8,128)(2,1)}, u32[]{:S(2)}, u32[]{:S(2)}) %collective-permute-start) | collective-permute-done | bytes 1048608 | tf_op jit(solution)/shard_map/ppermute | solution.py:15
  672.8 11.3 %collective-permute-done.1 = bf16[512,1024]{1,0:T(8,128)(2,1)} collective-permute-done((bf16[512,1024]{1,0:T(8,128)(2,1)S(1)}, bf16[512,1024]{1,0:T(8,128)(2,1)}, u32[]{:S(2)}, u32[]{:S(2)}) %collective-permute-start.1) | collective-permute-done | bytes 1048608 | tf_op jit(solution)/shard_map/ppermute | solution.py:15
  684.1 3.0 pad_maximum_fusion.1
  687.1 4.9 copy.80
  692.0 13.9 %fusion = (f32[4,2,512]{2,1,0:T(2,128)S(1)}, f32[4,1536,512,2]{2,1,3,0:T(8,128)}) fusion(pred[512,1536]{0,1:T(8,128)(4,1)S(1)} %copy-done.7, f32[512,4,2,256]{3,2,1,0:T(2,128)} %reshape.174, f32[256]{0:T(256)S(1)} %bitcast.124, f32[512,4,2]{0,2,1:T(2,128)S(1)} %rsqrt.30, bf16[512,4,256]{2,0,1:T(8,128)(2,1)S(1)} %bitcast.114, ...), kind=kOutput, calls=%fused_computation.3 | convolution fusion | flops 3252678656 | bytes 33326080 | tf_op jit(solution)/shard_map/tkgd,skd->kgts/dot_general | solution.py:146
  706.0 10.5 %fusion.12 = bf16[512,4,2,256]{0,3,2,1:T(8,128)(2,1)S(1)} fusion(bf16[1536,4,256,1]{0,2,3,1:T(8,128)(2,1)S(1)} %bitcast.112, f32[4,1536,512,2]{2,1,3,0:T(8,128)} %get-tuple-element.10, pred[512,1536]{0,1:T(8,128)(4,1)} %fusion.22, f32[512,4,2]{0,2,1:T(2,128)S(1)} %bitcast.125), kind=kOutput, calls=%fused_computation.22 | convolution fusion | flops 3242196992 | bytes 31211520 | tf_op jit(solution)/shard_map/kgts,skd->tkgd/dot_general | solution.py:152
  (71 shorter events, 47.5 us)
Async XLA Ops:
  6.5 83.7 %copy-start = (bf16[4,2560,48]{1,2,0:T(8,128)(2,1)S(1)}, bf16[4,2560,48]{1,2,0:T(8,128)(2,1)}, u32[]{:S(2)}) copy-start(bf16[4,2560,48]{1,2,0:T(8,128)(2,1)} %param.12) | copy-start | bytes 2949124
  90.3 1.5 copy-start.8
  106.0 126.0 %all-to-all-start.2 = ((bf16[16,4,16,4096]{3,2,1,0:T(8,128)(2,1)}), bf16[16,4,16,4096]{3,2,1,0:T(8,128)(2,1)}, u32[]{:S(2)}, u32[]{:S(2)}) async-start(bf16[16,4,16,4096]{3,2,1,0:T(8,128)(2,1)} %copy.62), calls=%async_computation.2 | async-start | bytes 16777216 | tf_op jit(solution)/shard_map/all_to_all | solution.py:105
  110.9 28.1 %all-gather.2.cloned.1.call-start = ((), (), s32[]{:S(2)}) async-start(), calls=%async_computation.3 | async-start | bytes 1474560 | tf_op jit(solution)/shard_map/all_gather | solution.py:76
  240.3 5.5 copy-start.10
  240.3 12.4 %copy-start.11 = (f32[2,256]{1,0:T(2,128)S(1)}, f32[2,256]{1,0:T(2,128)}, u32[]{:S(2)}) copy-start(f32[2,256]{1,0:T(2,128)} %param.11) | copy-start | bytes 6148
  240.3 324.3 %all-to-all-start = ((bf16[16,160,4096]{2,1,0:T(8,128)(2,1)}), bf16[16,160,4096]{2,1,0:T(8,128)(2,1)}, u32[]{:S(2)}, u32[]{:S(2)}) async-start(bf16[16,160,4096]{2,1,0:T(8,128)(2,1)} %stack.2), calls=%async_computation | async-start | bytes 41943040 | tf_op jit(solution)/shard_map/all_to_all | solution.py:80
  245.8 305.7 %collective-permute-start.2 = (s32[512]{0:T(512)S(1)}, s32[512]{0:T(512)S(1)}, u32[]{:S(2)}, u32[]{:S(2)}) collective-permute-start(s32[512]{0:T(512)S(1)} %copy-done.10), channel_id=1, source_target_pairs={{0,2},{1,3},{2,4},{3,5},{4,6},{5,7},{6,8},{7,9},{8,10},{9,11},{10,... | collective-permute-start | bytes 6152 | tf_op jit(solution)/shard_map/ppermute | solution.py:15
  250.4 301.1 %collective-permute-start.3 = (s32[512]{0:T(512)S(1)}, s32[512]{0:T(512)S(1)}, u32[]{:S(2)}, u32[]{:S(2)}) collective-permute-start(s32[512]{0:T(512)S(1)} %copy-done.10), channel_id=1, source_target_pairs={{0,1},{1,2},{2,3},{3,4},{4,5},{5,6},{6,7},{7,8},{8,9},{9,10},{10,1... | collective-permute-start | bytes 6152 | tf_op jit(solution)/shard_map/ppermute | solution.py:15
  551.5 13.1 %copy-start.9 = (f32[2560]{0:T(1024)S(1)}, f32[2560]{0:T(1024)}, u32[]{:S(2)}) copy-start(f32[2560]{0:T(1024)} %param.9) | copy-start | bytes 30724
  581.5 3.2 copy-start.2
  589.7 7.7 %copy-start.3 = (f32[512,4096]{1,0:T(8,128)S(1)}, f32[512,4096]{1,0:T(8,128)}, u32[]{:S(2)}) copy-start(f32[512,4096]{1,0:T(8,128)} %copy-done.2) | copy-start | bytes 25165828
  592.4 62.3 %collective-permute-start.5 = (bf16[512,1024]{1,0:T(8,128)(2,1)S(1)}, bf16[512,1024]{1,0:T(8,128)(2,1)}, u32[]{:S(2)}, u32[]{:S(2)}) collective-permute-start(bf16[512,1024]{1,0:T(8,128)(2,1)S(1)} %multiply_convert_fusion), channel_id=1, source_target_pairs={{0,1},{1,2},{2,3},{3,4},{4,5},{5,6},{6,7},{7,8},{8,9},{9,10},{10,1... | collective-permute-start | bytes 3145736 | tf_op jit(solution)/shard_map/ppermute | solution.py:15
  594.5 67.1 %collective-permute-start.4 = (bf16[512,1024]{1,0:T(8,128)(2,1)S(1)}, bf16[512,1024]{1,0:T(8,128)(2,1)}, u32[]{:S(2)}, u32[]{:S(2)}) collective-permute-start(bf16[512,1024]{1,0:T(8,128)(2,1)S(1)} %multiply_convert_fusion), channel_id=1, source_target_pairs={{0,2},{1,3},{2,4},{3,5},{4,6},{5,7},{6,8},{7,9},{8,10},{9,11},{10,... | collective-permute-start | bytes 3145736 | tf_op jit(solution)/shard_map/ppermute | solution.py:15
  597.5 75.3 %collective-permute-start = (bf16[512,1024]{1,0:T(8,128)(2,1)S(1)}, bf16[512,1024]{1,0:T(8,128)(2,1)}, u32[]{:S(2)}, u32[]{:S(2)}) collective-permute-start(bf16[512,1024]{1,0:T(8,128)(2,1)S(1)} %slice.85), channel_id=1, source_target_pairs={{0,2},{1,3},{2,4},{3,5},{4,6},{5,7},{6,8},{7,9},{8,10},{9,11},{10,... | collective-permute-start | bytes 3145736 | tf_op jit(solution)/shard_map/ppermute | solution.py:15
  600.4 83.7 %collective-permute-start.1 = (bf16[512,1024]{1,0:T(8,128)(2,1)S(1)}, bf16[512,1024]{1,0:T(8,128)(2,1)}, u32[]{:S(2)}, u32[]{:S(2)}) collective-permute-start(bf16[512,1024]{1,0:T(8,128)(2,1)S(1)} %slice.85), channel_id=1, source_target_pairs={{0,1},{1,2},{2,3},{3,4},{4,5},{5,6},{6,7},{7,8},{8,9},{9,10},{10,1... | collective-permute-start | bytes 3145736 | tf_op jit(solution)/shard_map/ppermute | solution.py:15
  687.1 4.9 copy-start.5
  687.1 4.9 copy-start.6
  687.1 4.9 copy-start.7
  692.0 13.9 %copy-start.4 = (bf16[1536,1024]{0,1:T(8,128)(2,1)S(1)}, bf16[1536,1024]{0,1:T(8,128)(2,1)}, u32[]{:S(2)}) copy-start(bf16[1536,1024]{0,1:T(8,128)(2,1)} %copy.80) | copy-start | bytes 9437188
  705.9 12.9 %copy-start.1 = (bf16[4,2560,48]{1,2,0:T(8,128)(2,1)S(1)}, bf16[4,2560,48]{1,2,0:T(8,128)(2,1)}, u32[]{:S(2)}) copy-start(bf16[4,2560,48]{1,2,0:T(8,128)(2,1)} %param.12) | copy-start | bytes 2949124
Sparse Core Ops, SparseCore 0:
  113.4 25.4 all-gather.1
